TPU v7x, 32 devices: a whole 2x2x4 slice. The times are simulated.
32 devices in a mesh: seq: 4 (over z), ctx: 8 (over y, x, core).
Axes of the slice: x: 2, y: 2, z: 4, core: 2. Of those that a mesh axis runs over, the one named last changes fastest.
Arguments:
- queries: bfloat16 [4, 4096, 2048], P('seq', 'ctx'), may hold values from -64 to 64
- keys: bfloat16 [4, 4096, 2048], P('seq', 'ctx'), may hold values from -6 to 6
- values: bfloat16 [4, 4096, 2048], P('seq', 'ctx'), may hold values from -6 to 6
- out_grad: bfloat16 [4, 4096, 2048], P('seq', 'ctx'), may hold values from -6 to 6
- cluster_ids: int32 [4, 16, 4096, 1], P('seq', None, 'ctx'), may hold values from 0 to 63; in each aligned block of 512 rows (0 to 511, 512 to 1023, ..., all dimensions but the last counted through in order) at most 16 rows name the same one
- centroids: float32 [16, 64, 128], replicated, may hold values from -6 to 6
Outputs:
- grad_queries: bfloat16 [4, 4096, 2048], P('seq', 'ctx')
- grad_keys: bfloat16 [4, 4096, 2048], P('seq', 'ctx')
- grad_values: bfloat16 [4, 4096, 2048], P('seq', 'ctx')
- new_centroids: float32 [16, 64, 128], P('ctx')
Inputs may be any that keep to these rules, and one draw needn't show every extreme that they name: `cluster_ids`: in each sequence and head, no cluster holds more than 16 of the 512 tokens of one index of ctx; some cluster holds exactly 16 in some such block.
All inputs are finite; a program needn't handle non-finite values.
Results may differ from a plain program's by a relative error of at most 0.0052.
Values may be sent and summed in bfloat16 or wider, within the bound.
A program may use at most 192 MiB of HBM per device.

v0:
```python
import math

import jax
import jax.numpy as jnp
from jax import lax
from jax.sharding import PartitionSpec as P

decay_rate = 0.99


def cluster_grads(packed, live_mask):
    head_width = packed.shape[-1] // 4
    score_scale = 1.0 / math.sqrt(head_width)
    query_rows = packed[..., :head_width]
    key_rows = packed[..., head_width : 2 * head_width]
    value_rows = packed[..., 2 * head_width : 3 * head_width]
    grad_rows = packed[..., 3 * head_width :]
    slot_count = packed.shape[1]
    row_ids = lax.broadcasted_iota(jnp.int32, (slot_count, slot_count), 0)
    col_ids = lax.broadcasted_iota(jnp.int32, (slot_count, slot_count), 1)
    allowed = (col_ids <= row_ids)[None] & (live_mask[:, None, :] | (col_ids == row_ids)[None])
    scores = (
        jnp.einsum("gqd,gkd->gqk", query_rows, key_rows, preferred_element_type=jnp.float32)
        * score_scale
    )
    scores = jnp.where(allowed, scores, -1e30)
    row_max = jnp.max(scores, axis=-1, keepdims=True)
    weights_raw = jnp.exp(scores - row_max)
    probs_full = weights_raw / jnp.sum(weights_raw, axis=-1, keepdims=True)
    probs_low = probs_full.astype(jnp.bfloat16)
    attended = jnp.einsum("gqk,gkd->gqd", probs_low, value_rows, preferred_element_type=jnp.float32)
    row_delta = jnp.sum(grad_rows.astype(jnp.float32) * attended, axis=-1, keepdims=True)
    dprobs = jnp.einsum("gqd,gkd->gqk", grad_rows, value_rows, preferred_element_type=jnp.float32)
    dscores = (probs_full * (dprobs - row_delta)).astype(jnp.bfloat16)
    dquery = (
        jnp.einsum("gqk,gkd->gqd", dscores, key_rows, preferred_element_type=jnp.float32)
        * score_scale
    )
    grad_key = (
        jnp.einsum("gqk,gqd->gkd", dscores, query_rows, preferred_element_type=jnp.float32)
        * score_scale
    )
    dvalue = jnp.einsum("gqk,gqd->gkd", probs_low, grad_rows, preferred_element_type=jnp.float32)
    return jnp.concatenate([dquery, grad_key, dvalue], axis=-1).astype(jnp.bfloat16)


def run_pairs(packed, live_mask):
    pair_count = packed.shape[0]
    group_size = math.gcd(pair_count, 4)
    shaped = packed.reshape((pair_count // group_size, group_size) + packed.shape[1:])
    mask_groups = live_mask.reshape(pair_count // group_size, group_size, live_mask.shape[-1])
    result = lax.map(
        lambda blocks_in: cluster_grads(blocks_in[0], blocks_in[1]), (shaped, mask_groups)
    )
    return result.reshape((pair_count,) + result.shape[2:])


def slot_ranks(ids_rows, cluster_total, block_rows):
    onehot = (ids_rows[..., None] == jnp.arange(cluster_total, dtype=jnp.int32)).astype(jnp.int32)
    lead = ids_rows.shape[:-1]
    blocks = onehot.reshape(lead + (ids_rows.shape[-1] // block_rows, block_rows, cluster_total))
    before = jnp.cumsum(blocks, axis=-2) - blocks
    rank_in = jnp.sum(before * blocks, axis=-1).reshape(ids_rows.shape)
    return (onehot, rank_in)


def member_sums(onehot, packed, head_width):
    member = onehot.astype(jnp.bfloat16)
    sums_two = jnp.einsum(
        "hlc,hld->hcd", member, packed[..., : 2 * head_width], preferred_element_type=jnp.float32
    )
    return sums_two[..., :head_width] + sums_two[..., head_width:]


def shards(queries, keys, values, out_grad, cluster_ids, centroids):
    tok_rows = queries.shape[1]
    head_count = cluster_ids.shape[1]
    head_width = queries.shape[2] // head_count
    cluster_total = centroids.shape[1]
    ctx_count = lax.axis_size("ctx")
    cap_rows = 2 * tok_rows // cluster_total
    own_heads = head_count // ctx_count
    stacked = jnp.concatenate(
        [
            source_arr[0].reshape(tok_rows, head_count, head_width)
            for source_arr in (queries, keys, values, out_grad)
        ],
        axis=-1,
    )
    packed = jnp.transpose(stacked, (1, 0, 2))
    ids_local = cluster_ids[0, :, :, 0]
    arrived, ids_arrived = (
        lax.all_to_all(packed, "ctx", split_axis=0, concat_axis=1, tiled=True),
        lax.all_to_all(
            ids_local.astype(jnp.bfloat16)[:, :, None],
            "ctx",
            split_axis=0,
            concat_axis=1,
            tiled=True,
        ),
    )
    ids_head = ids_arrived[..., 0].astype(jnp.int32)
    onehot, rank_in = slot_ranks(ids_head, cluster_total, tok_rows)
    slot_rows = ctx_count * cap_rows
    source = lax.broadcasted_iota(jnp.int32, ids_head.shape, 1) // tok_rows
    slot_of = ids_head * slot_rows + source * cap_rows + rank_in
    head_idx = lax.broadcasted_iota(jnp.int32, ids_head.shape, 0)
    buffers = (
        jnp.zeros((own_heads, cluster_total * slot_rows, 4 * head_width), jnp.bfloat16)
        .at[head_idx, slot_of]
        .set(arrived)
    )
    live = (
        jnp.zeros((own_heads, cluster_total * slot_rows), jnp.bool_).at[head_idx, slot_of].set(True)
    )
    grads = run_pairs(buffers.reshape(-1, slot_rows, 4 * head_width), live.reshape(-1, slot_rows))
    grads = grads.reshape(own_heads, cluster_total * slot_rows, 3 * head_width)
    back_rows = grads[head_idx, slot_of]
    grads_tok = lax.all_to_all(back_rows, "ctx", split_axis=1, concat_axis=0, tiled=True)
    sums_own = lax.psum(
        member_sums(onehot, arrived, head_width).astype(jnp.bfloat16), "seq"
    ).astype(jnp.float32)
    start_head = lax.axis_index("ctx") * own_heads
    centroid_own = lax.dynamic_slice_in_dim(centroids, start_head, own_heads, 0)
    updated = decay_rate * centroid_own + (1.0 - decay_rate) / 2.0 * sums_own
    per_token = jnp.transpose(grads_tok, (1, 0, 2))
    grad_queries = per_token[..., :head_width].reshape(1, tok_rows, head_count * head_width)
    grad_keys = per_token[..., head_width : 2 * head_width].reshape(
        1, tok_rows, head_count * head_width
    )
    grad_values = per_token[..., 2 * head_width :].reshape(1, tok_rows, head_count * head_width)
    return (grad_queries, grad_keys, grad_values, updated)


def solution(mesh):
    placed = (
        P("seq", "ctx", None),
        P("seq", "ctx", None),
        P("seq", "ctx", None),
        P("seq", "ctx", None),
        P("seq", None, "ctx", None),
        P(),
    )
    return jax.shard_map(
        shards,
        mesh=mesh,
        in_specs=placed,
        out_specs=(
            P("seq", "ctx", None),
            P("seq", "ctx", None),
            P("seq", "ctx", None),
            P("ctx", None, None),
        ),
        check_vma=False,
    )
```

profile of v0, /device:TPU:0, one launch (start us, length us, event | category | flops | bytes accessed | tf_op | source)
XLA Modules:
  0.0 565.8 jit_solution(2026954139724704129)
XLA Ops:
  3.3 5.2 all-to-all-start
  8.5 2.9 copy.139
  11.4 3.9 copy.140
  15.3 3.9 copy.141
  19.2 3.9 copy.142
  23.1 6.4 %maximum_bitcast_fusion = bf16[16,512,512]{1,2,0:T(8,128)(2,1)} fusion(bf16[512,16,128]{0,2,1:T(8,128)(2,1)} %bitcast.136, bf16[512,16,128]{0,2,1:T(8,128)(2,1)} %bitcast.135, bf16[512,16,128]{0,2,1:T(8,128)(2,1)} %bitcast.134, bf16[512,16,128]{0,2,1:T(8,128)(2,1)S(1)} %bitcast.133), kind=kLoop, calls=%fused_computation.37 | loop fusion | flops 33554432 | bytes 16777216 | tf_op jit(solution)/shard_map/transpose | solution.py:90
  29.5 5.0 all-to-all-start.1
  34.7 1.6 fusion.30
  36.4 34.0 %reduce-window.6 = s32[2,8,64,4,128]{4,2,3,1,0:T(8,128)S(1)} reduce-window(s32[2,8,64,4,128]{4,2,3,1,0:T(8,128)} %fusion.30, s32[]{:T(128)} %constant.39.clone.1), window={size=1x1x1x1x128 pad=0_0x0_0x0_0x0_0x127_0}, to_apply=%region_0.0 | reduce-window | flops 66584576 | bytes 4194308 | tf_op jit(solution)/shard_map/reduce-window
  70.4 1.9 slice.50
  72.3 2.3 copy.136
  76.0 34.8 %scatter_custom_fusion = pred[16384]{0:T(1024)(128)(4,1)S(1)} fusion(s32[8192]{0:T(1024)S(1)} %bitcast.144, pred[8192]{0:T(1024)(128)(4,1)S(1)} %broadcast.187, pred[]{:T(512)} %constant.66.clone.1), kind=kCustom, calls=%fused_computation.69 | custom fusion | bytes 16385
  110.8 17.7 %all-to-all-done.1 = bf16[16,512,512]{1,2,0:T(8,128)(2,1)} async-done(((bf16[16,512,512]{1,2,0:T(8,128)(2,1)}), bf16[16,512,512]{1,2,0:T(8,128)(2,1)}, u32[]{:S(2)}, u32[]{:S(2)}) %all-to-all-start.1) | async-done | bytes 8388640 | tf_op jit(solution)/shard_map/all_to_all | solution.py:93
  128.5 11.9 %copy.144 = bf16[2,8,512,512]{3,2,1,0:T(8,128)(2,1)} copy(bf16[2,8,512,512]{2,3,0,1:T(8,128)(2,1)} %bitcast.22) | data formatting | bytes 16777216 | tf_op jit(solution)/shard_map/all_to_all | solution.py:93
  140.4 45.1 %scatter_custom_fusion.1 = bf16[16384,512]{1,0:T(8,128)(2,1)} fusion(s32[8192]{0:T(1024)S(1)} %bitcast.145, bf16[8192,512]{1,0:T(8,128)(2,1)} %bitcast.128, bf16[]{:T(256)} %constant.58.clone.1), kind=kCustom, calls=%fused_computation.38 | custom fusion | bytes 16777728
  185.5 127.5 %while.10 = (s32[]{:T(128)}, bf16[32,4,128,384]{3,2,1,0:T(8,128)(2,1)}, pred[32,4,128]{2,1,0:T(4,128)(4,1)S(1)}, bf16[32,4,128,512]{3,2,1,0:T(8,128)(2,1)}, s32[]{:T(128)}) while((s32[]{:T(128)}, bf16[32,4,128,384]{3,2,1,0:T(8,128)(2,1)}, pred[32,4,128]{2,1,0:T(4,128)(4,1)S(1)}, bf16[32,4,128,512]{3,2,1,0:T(8,128)(2,1)}, s32[]{:T(128)}) %tuple.40), condition=%wide.region_9.10_spmd, body=%wide.region_5.9_spmd.sunk | while | flops 103449472 | bytes 7550545 | solution.py:52
  185.5 1.1 dynamic-slice_bitcast_fusion.4
  189.5 1.1 dynamic-slice_bitcast_fusion.4
  193.5 1.1 dynamic-slice_bitcast_fusion.4
  197.4 1.1 dynamic-slice_bitcast_fusion.4
  201.4 1.1 dynamic-slice_bitcast_fusion.4
  205.4 1.1 dynamic-slice_bitcast_fusion.4
  209.4 1.1 dynamic-slice_bitcast_fusion.4
  213.4 1.1 dynamic-slice_bitcast_fusion.4
  217.4 1.1 dynamic-slice_bitcast_fusion.4
  221.3 1.1 dynamic-slice_bitcast_fusion.4
  225.3 1.1 dynamic-slice_bitcast_fusion.4
  229.3 1.1 dynamic-slice_bitcast_fusion.4
  233.2 1.1 dynamic-slice_bitcast_fusion.4
  237.2 1.1 dynamic-slice_bitcast_fusion.4
  241.2 1.1 dynamic-slice_bitcast_fusion.4
  245.2 1.1 dynamic-slice_bitcast_fusion.4
  249.2 1.1 dynamic-slice_bitcast_fusion.4
  253.2 1.1 dynamic-slice_bitcast_fusion.4
  257.2 1.1 dynamic-slice_bitcast_fusion.4
  261.2 1.1 dynamic-slice_bitcast_fusion.4
  265.1 1.1 dynamic-slice_bitcast_fusion.4
  269.1 1.1 dynamic-slice_bitcast_fusion.4
  273.1 1.1 dynamic-slice_bitcast_fusion.4
  277.1 1.1 dynamic-slice_bitcast_fusion.4
  281.1 1.1 dynamic-slice_bitcast_fusion.4
  285.1 1.1 dynamic-slice_bitcast_fusion.4
  289.1 1.1 dynamic-slice_bitcast_fusion.4
  293.1 1.1 dynamic-slice_bitcast_fusion.4
  297.1 1.1 dynamic-slice_bitcast_fusion.4
  301.1 1.1 dynamic-slice_bitcast_fusion.4
  305.0 1.1 dynamic-slice_bitcast_fusion.4
  309.0 1.1 dynamic-slice_bitcast_fusion.4
  313.0 140.0 %gather_fusion = bf16[8192,384]{1,0:T(8,128)(2,1)} fusion(bf16[2,8192,384]{2,1,0:T(8,128)(2,1)} %bitcast.123, s32[8192]{0:T(1024)S(1)} %bitcast.122), kind=kCustom, calls=%fused_computation | custom fusion | bytes 12648448 | tf_op jit(solution)/shard_map/gather | solution.py:118
  453.0 12.7 %copy.146 = bf16[2,4096,384]{2,0,1:T(2,128)(2,1)} copy(bf16[2,4096,384]{2,1,0:T(8,128)(2,1)} %bitcast.125) | data formatting | bytes 12582912 | tf_op jit(solution)/shard_map/gather | solution.py:118
  465.7 4.8 all-to-all-start.2
  470.5 3.0 fusion.25
  473.6 19.3 %psum.7 = bf16[2,64,128]{2,1,0:T(8,128)(2,1)S(1)} all-reduce(bf16[2,64,128]{2,1,0:T(8,128)(2,1)S(1)} %fusion.32), channel_id=1, replica_groups=mesh['seq'=4,'ctx'=8] {'seq'}, use_global_device_ids=true, to_apply=%region_10.11 | all-reduce | flops 16384 | bytes 65536 | tf_op jit(solution)/shard_map/psum | solution.py:120
  492.9 1.5 multiply_add_fusion
  494.3 47.7 %all-to-all-done.2 = bf16[2,4096,384]{2,0,1:T(2,128)(2,1)} async-done(((bf16[2,4096,384]{2,0,1:T(2,128)(2,1)}), bf16[2,4096,384]{2,0,1:T(2,128)(2,1)}, u32[]{:S(2)}, u32[]{:S(2)}) %all-to-all-start.2) | async-done | bytes 6291488 | tf_op jit(solution)/shard_map/all_to_all | solution.py:119
  542.0 3.6 copy.147
  545.6 0.9 copy.148
  546.5 3.6 fusion.42
  550.1 2.9 copy.151
  552.9 2.4 copy.155
  555.3 2.9 copy.150
  558.2 2.4 copy.154
  560.6 2.9 copy.149
  563.4 2.4 copy.153
  (419 shorter events, 95.0 us)
Async XLA Ops:
  3.3 26.2 %all-to-all-start = ((bf16[8,2,512]{2,1,0:T(2,128)(2,1)}), bf16[8,2,512]{2,1,0:T(2,128)(2,1)S(1)}, u32[]{:S(2)}, u32[]{:S(2)}) async-start(bf16[8,2,512]{2,1,0:T(2,128)(2,1)} %reshape.281), calls=%async_computation | async-start | bytes 32768 | tf_op jit(solution)/shard_map/all_to_all | solution.py:94
  29.5 99.0 %all-to-all-start.1 = ((bf16[16,512,512]{1,2,0:T(8,128)(2,1)}), bf16[16,512,512]{1,2,0:T(8,128)(2,1)}, u32[]{:S(2)}, u32[]{:S(2)}) async-start(bf16[16,512,512]{1,2,0:T(8,128)(2,1)} %maximum_bitcast_fusion), calls=%async_computation.1 | async-start | bytes 16777216 | tf_op jit(solution)/shard_map/all_to_all | solution.py:93
  70.3 5.4 copy-start.1
  70.4 5.5 copy-start
  465.7 76.3 %all-to-all-start.2 = ((bf16[2,4096,384]{2,0,1:T(2,128)(2,1)}), bf16[2,4096,384]{2,0,1:T(2,128)(2,1)}, u32[]{:S(2)}, u32[]{:S(2)}) async-start(bf16[2,4096,384]{2,0,1:T(2,128)(2,1)} %copy.146), calls=%async_computation.2 | async-start | bytes 12582912 | tf_op jit(solution)/shard_map/all_to_all | solution.py:119
where the time goes:
time: 573 us; the launch traced here: 566 us
  local copies, waits for them, and re-layouts  356 us (62%)
  waiting for transfers between devices  65.4 us (11%)
  other arithmetic  55.9 us (10%)
  matrix products  51.5 us (9%)
  blocking collectives  19.3 us (3%)
  starting transfers between devices  14.9 us (3%)
    gather x2, local copies, waits for them, and re-layouts, shards(): back_rows = grads[head_idx, slot_of]  153 us
    unnamed x20, local copies, waits for them, and re-layouts  103 us
    all_to_all x1, waiting for transfers between devices, shards(): lax.all_to_all(back_rows, 'ctx', split_axis=1, concat_axis=0, tiled=True)  47.7 us
    squeeze x32, local copies, waits for them, and re-layouts, run_pairs(): lax.map(lambda blocks_in: cluster_grads(blocks_in[0], blocks_in[1]), (sha...  34.6 us
    another operation x2, other arithmetic  34.2 us
    dynamic_update_slice x64, local copies, waits for them, and re-layouts, run_pairs(): lax.map(lambda blocks_in: cluster_grads(blocks_in[0], blocks_in[1]), (sha...  32.7 us
    psum x1, blocking collectives, shards(): lax.psum(member_sums(onehot, arrived, head_width).astype(jnp.bfloat16), '...  19.3 us
    all_to_all x1, waiting for transfers between devices, shards(): lax.all_to_all(packed, 'ctx', split_axis=0, concat_axis=1, tiled=True)  17.7 us
  transfers between devices with their start and end apart: 3, of which 2 were waited for; matrix products, arithmetic and copies ran while one was open for 18% of the time, Pallas kernels for 0%

commit v1 on v0

v1 whole, which is shorter than its diff:
```python
import functools
import math

import jax
import jax.numpy as jnp
from jax import lax
from jax.experimental import pallas as pl
from jax.experimental.pallas import tpu as pltpu
from jax.sharding import PartitionSpec as P

decay_rate = 0.99
NEG = -1e30


def dot(a, b, ca=1, cb=0):
    return lax.dot_general(a, b, (((ca,), (cb,)), ((), ())), preferred_element_type=jnp.float32)


def iota(shape, dim):
    return lax.broadcasted_iota(jnp.int32, shape, dim)


def fill_tables(upper, causal):
    upper[...] = jnp.where(iota(upper.shape, 0) < iota(upper.shape, 1), 1.0, 0.0).astype(jnp.bfloat16)
    causal[...] = jnp.where(iota(causal.shape, 0) <= iota(causal.shape, 1), 0.0, NEG)


def expand_block(rows, ids_row, at, upper, slots, bias, slot_col):
    clusters, _, width = slots.shape
    tok = ids_row.shape[1]
    cap = 2 * tok // clusters
    head = width // 4
    hit = iota((clusters, tok), 0) == ids_row
    onehot = jnp.where(hit, 1.0, 0.0).astype(jnp.bfloat16)
    before = dot(onehot, upper[...])
    rank = jnp.sum(jnp.where(hit, before, 0.0), axis=0, keepdims=True)
    slot = ids_row * cap + rank.astype(jnp.int32)
    for i in range(tok // 128):
        piece = jnp.where(iota((128, 128), 0) == iota((128, 128), 1), slot[:, i * 128 : (i + 1) * 128], 0)
        col = jnp.sum(piece.astype(jnp.float32), axis=1, keepdims=True)
        slot_col[pl.ds(i * 128, 128), :] = jnp.broadcast_to(col, (128, 128)).astype(jnp.int32)
    group = min(clusters, 256 // cap)
    where_to = pl.ds(pl.multiple_of(at * cap, cap), cap)
    for i in range(clusters // group):
        take = jnp.where(iota((group * cap, tok), 0) + i * group * cap == slot, 1.0, 0.0)
        live = jnp.sum(take, axis=1, keepdims=True)
        placed = dot(take.astype(jnp.bfloat16), rows).astype(jnp.bfloat16)
        slots[pl.ds(i * group, group), where_to, :] = placed.reshape(group, cap, width)
        hide = jnp.broadcast_to(jnp.where(live > 0.5, 0.0, NEG), (group * cap, 128))
        bias[pl.ds(i * group, group), where_to, :] = hide.reshape(group, cap, 128)
    sums = dot(onehot, rows[:, : 2 * head])
    return sums[:, :head] + sums[:, head:]


def attend(slots, bias, causal, step):
    clusters, count, width = slots.shape
    head = width // 4
    scale = 1.0 / math.sqrt(head)

    def some(i, carry):
        at = [i * step + j for j in range(step)]
        q = [slots[c, :, :head] for c in at]
        k = [slots[c, :, head : 2 * head] for c in at]
        v = [slots[c, :, 2 * head : 3 * head] for c in at]
        g = [slots[c, :, 3 * head :] for c in at]
        hide = [jnp.concatenate([bias[c]] * (count // 128), axis=1) for c in at]
        s = [dot(b, a, 1, 1) for a, b in zip(q, k)]
        dp = [dot(b, a, 1, 1) for a, b in zip(g, v)]
        s = [a * scale + causal[...] + b for a, b in zip(s, hide)]
        e = [jnp.exp(a - jnp.max(a, axis=0, keepdims=True)) for a in s]
        p = [a * (1.0 / jnp.sum(a, axis=0, keepdims=True)) for a in e]
        low = [a.astype(jnp.bfloat16) for a in p]
        delta = [jnp.sum(a.astype(jnp.float32) * b, axis=0, keepdims=True) for a, b in zip(low, dp)]
        ds = [(a * (b - c)).astype(jnp.bfloat16) for a, b, c in zip(p, dp, delta)]
        dv = [dot(a, b).astype(jnp.bfloat16) for a, b in zip(low, g)]
        dk = [(dot(a, b) * scale).astype(jnp.bfloat16) for a, b in zip(ds, q)]
        dq = [(dot(a, b, 0, 0) * scale).astype(jnp.bfloat16) for a, b in zip(ds, k)]
        for j, c in enumerate(at):
            slots[c, :, :head] = dq[j]
            slots[c, :, head : 2 * head] = dk[j]
            slots[c, :, 2 * head : 3 * head] = dv[j]
        return carry

    lax.fori_loop(0, clusters // step, some, 0)


def collect_block(at, slots, slot_col, write):
    clusters, _, width = slots.shape
    tok = slot_col.shape[0]
    cap = 2 * tok // clusters
    keep = 3 * (width // 4)
    grads = slots[:, pl.ds(pl.multiple_of(at * cap, cap), cap), :keep].reshape(clusters * cap, keep)
    rows = min(tok, 256)
    for i in range(tok // rows):
        col = slot_col[pl.ds(i * rows, rows), :]
        col = jnp.concatenate([col] * (clusters * cap // 128), axis=1)
        take = jnp.where(col == iota((rows, clusters * cap), 1), 1.0, 0.0).astype(jnp.bfloat16)
        write(i * rows, dot(take, grads).astype(jnp.bfloat16))


def head_kernel(x, ids, out, sums, slots, bias, slot_col, upper, causal):
    n = x.shape[0]
    fill_tables(upper, causal)
    sums[...] = jnp.zeros_like(sums)

    def into(b, carry):
        sums[...] += expand_block(x[b], ids[b], b, upper, slots, bias, slot_col.at[b])
        return carry

    lax.fori_loop(0, n, into, 0)
    attend(slots, bias, causal, 4)

    def back(b, carry):
        def write(first, rows):
            out[b, pl.ds(first, rows.shape[0]), :] = rows

        collect_block(b, slots, slot_col.at[b], write)
        return carry

    lax.fori_loop(0, n, back, 0)


def head_grads(x, ids, clusters):
    n, tok, width = x.shape
    head = width // 4
    count = n * (2 * tok // clusters)
    vmem = pl.BlockSpec(memory_space=pltpu.VMEM)
    return pl.pallas_call(
        head_kernel,
        out_shape=(
            jax.ShapeDtypeStruct((n, tok, 3 * head), jnp.bfloat16),
            jax.ShapeDtypeStruct((clusters, head), jnp.float32),
        ),
        in_specs=[vmem, vmem],
        out_specs=(vmem, vmem),
        scratch_shapes=[
            pltpu.VMEM((clusters, count, width), jnp.bfloat16),
            pltpu.VMEM((clusters, count, 128), jnp.float32),
            pltpu.VMEM((n, tok, 128), jnp.int32),
            pltpu.VMEM((tok, tok), jnp.bfloat16),
            pltpu.VMEM((count, count), jnp.float32),
        ],
        compiler_params=pltpu.CompilerParams(vmem_limit_bytes=60 * 1024 * 1024),
        cost_estimate=pl.CostEstimate(flops=30_000_000_000, bytes_accessed=8 << 20, transcendentals=0),
    )(x, ids)


def shards(queries, keys, values, out_grad, cluster_ids, centroids):
    tok = queries.shape[1]
    heads = cluster_ids.shape[1]
    head = queries.shape[2] // heads
    clusters = centroids.shape[1]
    n = lax.axis_size("ctx")
    seqs = lax.axis_size("seq")
    own = heads // n
    a2a = functools.partial(lax.all_to_all, axis_name="ctx", split_axis=0, concat_axis=0, tiled=True)
    ids = a2a(cluster_ids.reshape(n, own, tok)).reshape(n, own, 1, tok)
    split = [a[0].reshape(tok, n, own, head) for a in (queries, keys, values, out_grad)]
    arrived = [
        a2a(jnp.transpose(jnp.concatenate([a[:, :, h] for a in split], axis=-1), (1, 0, 2)))
        for h in range(own)
    ]
    done = [head_grads(arrived[h], ids[:, h], clusters) for h in range(own)]
    back = jnp.stack([a2a(d[0]) for d in done], axis=1)
    sums = jnp.stack([d[1] for d in done]).astype(jnp.bfloat16)
    total = sums.astype(jnp.float32)
    for d in range(1, seqs):
        moved = lax.ppermute(sums, "seq", [(i, (i + d) % seqs) for i in range(seqs)])
        total = total + moved.astype(jnp.float32)
    centroid_own = lax.dynamic_slice_in_dim(centroids, lax.axis_index("ctx") * own, own, 0)
    updated = decay_rate * centroid_own + (1.0 - decay_rate) / 2.0 * total
    per_token = jnp.transpose(back, (2, 0, 1, 3))
    grads = [
        per_token[..., i * head : (i + 1) * head].reshape(1, tok, heads * head) for i in range(3)
    ]
    return (*grads, updated)


def solution(mesh):
    split = P("seq", "ctx", None)
    return jax.shard_map(
        shards,
        mesh=mesh,
        in_specs=(split, split, split, split, P("seq", None, "ctx", None), P()),
        out_specs=(split, split, split, P("ctx", None, None)),
        check_vma=False,
    )
```

time: 573 us -> 251 us (0.44); the launches traced: 566 us -> 250 us
  local copies, waits for them, and re-layouts: 356 us -> 50.9 us
  Pallas kernels: 0 us -> 54.1 us
  matrix products: 51.5 us -> 0 us
  other arithmetic: 55.9 us -> 11.9 us
  waiting for transfers between devices: 65.4 us -> 103 us
  blocking collectives: 19.3 us -> 0 us
  starting transfers between devices: 14.9 us -> 29 us
    gather x2 -> x0, local copies, waits for them, and re-layouts: 153 us -> none  [shards(): back_rows = grads[head_idx, slot_of]]
    unnamed x20 -> x27, local copies, waits for them, and re-layouts: 103 us -> 31.6 us
    pallas_call x0 -> x2, Pallas kernels: none -> 54.1 us  [head_grads(): pl.pallas_call(head_kernel, out_shape=(jax.ShapeDtypeStruct((n, tok, 3 *...]
    dot_general x193 -> x0, matrix products: 51.5 us -> none  [the longest x32 11.8 us: cluster_grads(): jnp.einsum('gqk,gkd->gqd', probs_low, value_rows, preferred_element_type=...]
    all_to_all x3 -> x5, waiting for transfers between devices: 65.4 us -> 101 us  [the longest x2 62.5 us: shards(): a2a(jnp.transpose(jnp.concatenate([a[:, :, h] for a in split], axis=-1),...]
    another operation x2 -> x3, other arithmetic: 34.2 us -> 0.02 us  [shards(): sums = jnp.stack([d[1] for d in done]).astype(jnp.bfloat16)]
    squeeze x32 -> x1, local copies, waits for them, and re-layouts: 34.6 us -> 0.64 us  [shards(): done = [head_grads(arrived[h], ids[:, h], clusters) for h in range(own)]]
    dynamic_update_slice x64 -> x0, local copies, waits for them, and re-layouts: 32.7 us -> none  [run_pairs(): lax.map(lambda blocks_in: cluster_grads(blocks_in[0], blocks_in[1]), (sha...]
  transfers between devices with their start and end apart: 3 -> 8, of which waited for: 2 -> 5; matrix products, arithmetic and copies ran while one was open for 18% -> 16% of each run, Pallas kernels for 0% -> 22%
where the time goes in v1:
time: 251 us; the launch traced here: 250 us
  waiting for transfers between devices  103 us (41%)
  Pallas kernels  54.1 us (22%)
  local copies, waits for them, and re-layouts  50.9 us (20%)
  starting transfers between devices  29 us (12%)
  other arithmetic  11.9 us (5%)
    all_to_all x2, waiting for transfers between devices, shards(): a2a(jnp.transpose(jnp.concatenate([a[:, :, h] for a in split], axis=-1),...  62.5 us
    pallas_call x2, Pallas kernels, head_grads(): pl.pallas_call(head_kernel, out_shape=(jax.ShapeDtypeStruct((n, tok, 3 *...  54.1 us
    all_to_all x2, waiting for transfers between devices, shards(): back = jnp.stack([a2a(d[0]) for d in done], axis=1)  38.5 us
    unnamed x27, local copies, waits for them, and re-layouts  31.6 us
    slice x4, local copies, waits for them, and re-layouts, shards(): per_token[..., i * head:(i + 1) * head].reshape(1, tok, heads * head)  12.1 us
    all_to_all x2, starting transfers between devices, shards(): a2a(jnp.transpose(jnp.concatenate([a[:, :, h] for a in split], axis=-1),...  9.26 us
    all_to_all x2, starting transfers between devices, shards(): back = jnp.stack([a2a(d[0]) for d in done], axis=1)  8.1 us
    transpose x2, other arithmetic, shards(): jnp.transpose(jnp.concatenate([a[:, :, h] for a in split], axis=-1), (1,...  6.98 us
  transfers between devices with their start and end apart: 8, of which 5 were waited for; matrix products, arithmetic and copies ran while one was open for 16% of the time, Pallas kernels for 22%

profile of v1, /device:TPU:0, one launch (start us, length us, event | category | flops | bytes accessed | tf_op | source)
XLA Modules:
  0.0 249.7 jit_solution(5285709793391556699)
XLA Ops:
  0.6 0.8 reduce
  1.5 0.6 reshape.23
  2.1 5.2 %all-to-all-start.1 = ((s32[8,2,512]{2,1,0:T(2,128)}), s32[8,2,512]{2,1,0:T(2,128)S(1)}, u32[]{:S(2)}, u32[]{:S(2)}) async-start(s32[8,2,512]{2,1,0:T(2,128)} %reshape.23), calls=%async_computation.1 | async-start | bytes 65536 | tf_op jit(solution)/shard_map/all_to_all | solution.py:157
  7.3 2.9 %copy.10 = bf16[1,512,2048]{1,2,0:T(8,128)(2,1)S(1)} copy(bf16[1,512,2048]{2,1,0:T(8,128)(2,1)} %param.6) | data formatting | bytes 4194304 | tf_op args[0]
  10.2 1.2 fusion.1
  11.3 2.3 copy.29
  13.6 2.9 %copy.12 = bf16[1,512,2048]{1,2,0:T(8,128)(2,1)S(1)} copy(bf16[1,512,2048]{2,1,0:T(8,128)(2,1)} %param.7) | data formatting | bytes 4194304 | tf_op args[1]
  16.5 1.6 fusion.2
  18.1 2.2 copy.30
  20.3 2.9 %copy.14 = bf16[1,512,2048]{1,2,0:T(8,128)(2,1)S(1)} copy(bf16[1,512,2048]{2,1,0:T(8,128)(2,1)} %param.8) | data formatting | bytes 4194304 | tf_op args[2]
  23.2 1.5 fusion.3
  24.7 2.3 copy.31
  27.0 2.9 %copy.16 = bf16[1,512,2048]{1,2,0:T(8,128)(2,1)S(1)} copy(bf16[1,512,2048]{2,1,0:T(8,128)(2,1)} %param.9) | data formatting | bytes 4194304 | tf_op args[3]
  29.9 1.5 fusion.4
  31.4 1.6 copy.32
  33.0 3.6 %maximum_bitcast_fusion.1 = bf16[8,512,512]{2,1,0:T(8,128)(2,1)} fusion(bf16[512,8,128]{2,0,1:T(8,128)(2,1)S(1)} %bitcast.46, bf16[512,8,128]{2,0,1:T(8,128)(2,1)} %bitcast.42, bf16[512,8,128]{2,0,1:T(8,128)(2,1)} %bitcast.41, bf16[512,8,128]{2,0,1:T(8,128)(2,1)} %bitcast.40), kind=kLoop, calls=%fused_computation.1 | loop fusion | flops 16777216 | bytes 8388608 | tf_op jit(solution)/shard_map/transpose | solution.py:160
  36.6 0.0 copy-start
  36.6 0.0 all-to-all-done.1
  36.6 4.7 %all-to-all-start = ((bf16[8,512,512]{2,1,0:T(8,128)(2,1)}), bf16[8,512,512]{2,1,0:T(8,128)(2,1)}, u32[]{:S(2)}, u32[]{:S(2)}) async-start(bf16[8,512,512]{2,1,0:T(8,128)(2,1)} %maximum_bitcast_fusion.1), calls=%async_computation | async-start | bytes 8388608 | tf_op jit(solution)/shard_map/all_to_all | solution.py:160
  41.3 0.0 copy-start.1
  41.3 1.3 copy.33
  42.6 0.0 copy-start.2
  42.6 0.0 copy-done
  42.6 1.3 copy.34
  44.0 0.0 copy-start.3
  44.0 0.0 copy-done.1
  44.0 1.3 copy.35
  45.3 0.0 copy-done.2
  45.3 0.7 copy.36
  45.9 0.0 copy-done.3
  45.9 3.4 %maximum_bitcast_fusion.2 = bf16[8,512,512]{2,1,0:T(8,128)(2,1)} fusion(bf16[512,8,128]{2,0,1:T(8,128)(2,1)S(1)} %bitcast.47, bf16[512,8,128]{2,0,1:T(8,128)(2,1)} %bitcast.45, bf16[512,8,128]{2,0,1:T(8,128)(2,1)} %bitcast.44, bf16[512,8,128]{2,0,1:T(8,128)(2,1)S(1)} %bitcast.43), kind=kLoop, calls=%fused_computation.2 | loop fusion | flops 16777216 | bytes 8388608 | tf_op jit(solution)/shard_map/transpose | solution.py:160
  49.4 41.0 %all-to-all-done.x = bf16[8,512,512]{2,1,0:T(8,128)(2,1)} async-done(((bf16[8,512,512]{2,1,0:T(8,128)(2,1)}), bf16[8,512,512]{2,1,0:T(8,128)(2,1)}, u32[]{:S(2)}, u32[]{:S(2)}) %all-to-all-start) | async-done | bytes 4194336 | tf_op jit(solution)/shard_map/all_to_all | solution.py:160
  90.4 4.6 %all-to-all-start.3 = ((bf16[8,512,512]{2,1,0:T(8,128)(2,1)}), bf16[8,512,512]{2,1,0:T(8,128)(2,1)}, u32[]{:S(2)}, u32[]{:S(2)}) async-start(bf16[8,512,512]{2,1,0:T(8,128)(2,1)} %maximum_bitcast_fusion.2), calls=%async_computation.3 | async-start | bytes 8388608 | tf_op jit(solution)/shard_map/all_to_all | solution.py:160
  95.0 0.6 slice_bitcast_fusion.1
  95.6 27.0 %shard_map.93 = (bf16[8,512,384]{2,1,0:T(8,128)(2,1)}, f32[64,128]{1,0:T(8,128)}) custom-call(bf16[8,512,512]{2,1,0:T(8,128)(2,1)} %all-to-all-done.x, s32[8,1,512]{2,1,0:T(1,128)} %get-tuple-element.27.ids), custom_call_target="tpu_custom_call" | custom-call | flops 30000001024 | bytes 8388608 | tf_op jit(solution)/shard_map/pallas_call | solution.py:128
  122.6 21.5 %all-to-all-done.3.x = bf16[8,512,512]{2,1,0:T(8,128)(2,1)} async-done(((bf16[8,512,512]{2,1,0:T(8,128)(2,1)}), bf16[8,512,512]{2,1,0:T(8,128)(2,1)}, u32[]{:S(2)}, u32[]{:S(2)}) %all-to-all-start.3) | async-done | bytes 4194336 | tf_op jit(solution)/shard_map/all_to_all | solution.py:160
  144.1 3.6 %all-to-all-start.2 = ((bf16[8,512,384]{2,1,0:T(8,128)(2,1)}), bf16[8,512,384]{2,1,0:T(8,128)(2,1)S(1)}, u32[]{:S(2)}, u32[]{:S(2)}) async-start(bf16[8,512,384]{2,1,0:T(8,128)(2,1)} %get-tuple-element.8), calls=%async_computation.2 | async-start | bytes 6291456 | tf_op jit(solution)/shard_map/all_to_all | solution.py:164
  147.7 27.1 %shard_map.94 = (bf16[8,512,384]{2,1,0:T(8,128)(2,1)}, f32[64,128]{1,0:T(8,128)}) custom-call(bf16[8,512,512]{2,1,0:T(8,128)(2,1)} %all-to-all-done.3.x, s32[8,1,512]{2,1,0:T(1,128)} %get-tuple-element.28.ids), custom_call_target="tpu_custom_call" | custom-call | flops 30000001024 | bytes 8388608 | tf_op jit(solution)/shard_map/pallas_call | solution.py:128
  174.8 0.0 copy-start.4
  174.8 0.0 copy-start.5
  174.8 10.7 %all-to-all-done.2 = bf16[8,512,384]{2,1,0:T(8,128)(2,1)S(1)} async-done(((bf16[8,512,384]{2,1,0:T(8,128)(2,1)}), bf16[8,512,384]{2,1,0:T(8,128)(2,1)S(1)}, u32[]{:S(2)}, u32[]{:S(2)}) %all-to-all-start.2) | async-done | bytes 3145760 | tf_op jit(solution)/shard_map/all_to_all | solution.py:164
  185.5 4.4 %all-to-all-start.4 = ((bf16[8,512,384]{2,1,0:T(8,128)(2,1)}), bf16[8,512,384]{2,1,0:T(8,128)(2,1)}, u32[]{:S(2)}, u32[]{:S(2)}) async-start(bf16[8,512,384]{2,1,0:T(8,128)(2,1)} %get-tuple-element.9), calls=%async_computation.4 | async-start | bytes 6291456 | tf_op jit(solution)/shard_map/all_to_all | solution.py:164
  190.0 0.0 copy-done.4
  190.0 0.0 copy-done.5
  190.0 2.7 %collective-permute-start.1 = (bf16[2,64,128]{2,1,0:T(8,128)(2,1)S(1)}, bf16[2,64,128]{2,1,0:T(8,128)(2,1)S(1)}, u32[]{:S(2)}, u32[]{:S(2)}) collective-permute-start(bf16[2,64,128]{2,1,0:T(8,128)(2,1)S(1)} %pad_maximum_fusion), channel_id=1, source_target_pairs={{0,16},{8,24},{16,0},{24,8},{1,17},{9,25},{17,1},{25,9},{2,18},{10... | collective-permute-start | bytes 98312 | tf_op jit(solution)/shard_map/ppermute | solution.py:168
  192.7 1.6 collective-permute-start
  194.2 2.2 collective-permute-start.2
  196.5 0.0 collective-permute-done.1
  196.5 2.0 collective-permute-done
  198.5 0.0 collective-permute-done.2
  198.5 1.5 multiply_add_fusion
  200.0 27.8 %all-to-all-done.4 = bf16[8,512,384]{2,1,0:T(8,128)(2,1)} async-done(((bf16[8,512,384]{2,1,0:T(8,128)(2,1)}), bf16[8,512,384]{2,1,0:T(8,128)(2,1)}, u32[]{:S(2)}, u32[]{:S(2)}) %all-to-all-start.4) | async-done | bytes 3145760 | tf_op jit(solution)/shard_map/all_to_all | solution.py:164
  227.8 2.6 %maximum_bitcast_fusion = bf16[512,8,2,384]{3,0,1,2:T(8,128)(2,1)S(1)} fusion(bf16[8,1,512,384]{3,2,0,1:T(8,128)(2,1)} %bitcast.18, bf16[8,1,512,384]{3,2,0,1:T(8,128)(2,1)S(1)} %bitcast.32), kind=kLoop, calls=%fused_computation | loop fusion | flops 3145728 | bytes 12582912 | tf_op jit(solution)/shard_map/transpose | solution.py:172
  230.4 3.6 %fusion = (bf16[512,8,2,128]{3,0,1,2:T(8,128)(2,1)}, bf16[512,8,2,128]{3,0,1,2:T(8,128)(2,1)}, bf16[512,8,2,128]{3,0,1,2:T(8,128)(2,1)}) fusion(bf16[512,8,2,384]{3,0,1,2:T(8,128)(2,1)S(1)} %maximum_bitcast_fusion), kind=kLoop, calls=%fused_computation.9 | loop fusion | bytes 12582912 | tf_op jit(solution)/shard_map/slice | solution.py:174
  234.0 2.9 %copy.24 = bf16[512,8,2,128]{0,3,2,1:T(8,128)(2,1)S(1)} copy(bf16[512,8,2,128]{3,0,1,2:T(8,128)(2,1)} %get-tuple-element.16) | data formatting | bytes 4194304 | tf_op jit(solution)/shard_map/slice | solution.py:174
  236.8 2.4 copy.27
  239.2 2.9 %copy.23 = bf16[512,8,2,128]{0,3,2,1:T(8,128)(2,1)S(1)} copy(bf16[512,8,2,128]{3,0,1,2:T(8,128)(2,1)} %get-tuple-element.17) | data formatting | bytes 4194304 | tf_op jit(solution)/shard_map/slice | solution.py:174
  242.1 2.4 copy.26
  244.5 2.9 %copy.22 = bf16[512,8,2,128]{0,3,2,1:T(8,128)(2,1)S(1)} copy(bf16[512,8,2,128]{3,0,1,2:T(8,128)(2,1)} %get-tuple-element.18) | data formatting | bytes 4194304 | tf_op jit(solution)/shard_map/slice | solution.py:174
  247.3 2.4 copy.25
  (3 shorter events, 0.0 us)
Async XLA Ops:
  2.1 34.5 %all-to-all-start.1 = ((s32[8,2,512]{2,1,0:T(2,128)}), s32[8,2,512]{2,1,0:T(2,128)S(1)}, u32[]{:S(2)}, u32[]{:S(2)}) async-start(s32[8,2,512]{2,1,0:T(2,128)} %reshape.23), calls=%async_computation.1 | async-start | bytes 65536 | tf_op jit(solution)/shard_map/all_to_all | solution.py:157
  36.6 6.1 %copy-start = (bf16[512,8,1,128]{0,3,2,1:T(8,128)(2,1)S(1)}, bf16[512,8,1,128]{0,3,2,1:T(8,128)(2,1)}, u32[]{:S(2)}) copy-start(bf16[512,8,1,128]{0,3,2,1:T(8,128)(2,1)} %get-tuple-element.22) | copy-start | bytes 3145732
  36.6 53.8 %all-to-all-start = ((bf16[8,512,512]{2,1,0:T(8,128)(2,1)}), bf16[8,512,512]{2,1,0:T(8,128)(2,1)}, u32[]{:S(2)}, u32[]{:S(2)}) async-start(bf16[8,512,512]{2,1,0:T(8,128)(2,1)} %maximum_bitcast_fusion.1), calls=%async_computation | async-start | bytes 8388608 | tf_op jit(solution)/shard_map/all_to_all | solution.py:160
  41.3 2.7 %copy-start.1 = (bf16[512,8,1,128]{0,3,2,1:T(8,128)(2,1)S(1)}, bf16[512,8,1,128]{0,3,2,1:T(8,128)(2,1)}, u32[]{:S(2)}) copy-start(bf16[512,8,1,128]{0,3,2,1:T(8,128)(2,1)} %get-tuple-element.24) | copy-start | bytes 3145732
  42.6 2.6 %copy-start.2 = (bf16[512,8,1,128]{0,3,2,1:T(8,128)(2,1)S(1)}, bf16[512,8,1,128]{0,3,2,1:T(8,128)(2,1)}, u32[]{:S(2)}) copy-start(bf16[512,8,1,128]{0,3,2,1:T(8,128)(2,1)} %get-tuple-element.26) | copy-start | bytes 3145732
  44.0 2.0 copy-start.3
  90.4 53.7 %all-to-all-start.3 = ((bf16[8,512,512]{2,1,0:T(8,128)(2,1)}), bf16[8,512,512]{2,1,0:T(8,128)(2,1)}, u32[]{:S(2)}, u32[]{:S(2)}) async-start(bf16[8,512,512]{2,1,0:T(8,128)(2,1)} %maximum_bitcast_fusion.2), calls=%async_computation.3 | async-start | bytes 8388608 | tf_op jit(solution)/shard_map/all_to_all | solution.py:160
  144.1 41.4 %all-to-all-start.2 = ((bf16[8,512,384]{2,1,0:T(8,128)(2,1)}), bf16[8,512,384]{2,1,0:T(8,128)(2,1)S(1)}, u32[]{:S(2)}, u32[]{:S(2)}) async-start(bf16[8,512,384]{2,1,0:T(8,128)(2,1)} %get-tuple-element.8), calls=%async_computation.2 | async-start | bytes 6291456 | tf_op jit(solution)/shard_map/all_to_all | solution.py:164
  174.8 15.2 %copy-start.4 = (f32[64,128]{1,0:T(8,128)S(1)}, f32[64,128]{1,0:T(8,128)}, u32[]{:S(2)}) copy-start(f32[64,128]{1,0:T(8,128)} %get-tuple-element.10) | copy-start | bytes 98308
  174.8 15.2 %copy-start.5 = (f32[64,128]{1,0:T(8,128)S(1)}, f32[64,128]{1,0:T(8,128)}, u32[]{:S(2)}) copy-start(f32[64,128]{1,0:T(8,128)} %get-tuple-element.11) | copy-start | bytes 98308
  185.5 42.3 %all-to-all-start.4 = ((bf16[8,512,384]{2,1,0:T(8,128)(2,1)}), bf16[8,512,384]{2,1,0:T(8,128)(2,1)}, u32[]{:S(2)}, u32[]{:S(2)}) async-start(bf16[8,512,384]{2,1,0:T(8,128)(2,1)} %get-tuple-element.9), calls=%async_computation.4 | async-start | bytes 6291456 | tf_op jit(solution)/shard_map/all_to_all | solution.py:164
  190.0 6.5 %collective-permute-start.1 = (bf16[2,64,128]{2,1,0:T(8,128)(2,1)S(1)}, bf16[2,64,128]{2,1,0:T(8,128)(2,1)S(1)}, u32[]{:S(2)}, u32[]{:S(2)}) collective-permute-start(bf16[2,64,128]{2,1,0:T(8,128)(2,1)S(1)} %pad_maximum_fusion), channel_id=1, source_target_pairs={{0,16},{8,24},{16,0},{24,8},{1,17},{9,25},{17,1},{25,9},{2,18},{10... | collective-permute-start | bytes 98312 | tf_op jit(solution)/shard_map/ppermute | solution.py:168
  192.7 5.8 %collective-permute-start = (bf16[2,64,128]{2,1,0:T(8,128)(2,1)S(1)}, bf16[2,64,128]{2,1,0:T(8,128)(2,1)S(1)}, u32[]{:S(2)}, u32[]{:S(2)}) collective-permute-start(bf16[2,64,128]{2,1,0:T(8,128)(2,1)S(1)} %pad_maximum_fusion), channel_id=1, source_target_pairs={{0,8},{8,16},{16,24},{24,0},{1,9},{9,17},{17,25},{25,1},{2,10},{10... | collective-permute-start | bytes 98312 | tf_op jit(solution)/shard_map/ppermute | solution.py:168
  194.2 4.3 %collective-permute-start.2 = (bf16[2,64,128]{2,1,0:T(8,128)(2,1)S(1)}, bf16[2,64,128]{2,1,0:T(8,128)(2,1)S(1)}, u32[]{:S(2)}, u32[]{:S(2)}) collective-permute-start(bf16[2,64,128]{2,1,0:T(8,128)(2,1)S(1)} %pad_maximum_fusion), channel_id=1, source_target_pairs={{0,24},{8,0},{16,8},{24,16},{1,25},{9,1},{17,9},{25,17},{2,26},{10... | collective-permute-start | bytes 98312 | tf_op jit(solution)/shard_map/ppermute | solution.py:168

commit v2 on v1

--- a/solution.py
+++ b/solution.py
@@ -98,51 +98,144 @@
         write(i * rows, dot(take, grads).astype(jnp.bfloat16))
 
 
-def head_kernel(x, ids, out, sums, slots, bias, slot_col, upper, causal):
-    n = x.shape[0]
+def spread_kernel(n, seqs, own, *refs):
+    args, refs = refs[:4], refs[4:]
+    ids, grads, total, refs = refs[0], refs[1:4], refs[4], refs[5:]
+    (recv, recv_ids, ready, all_sums, sums, slots, bias, slot_col, upper, causal), refs = refs[:10], refs[10:]
+    local_sem, ids_local, out_send, out_recv, ids_send, ids_recv, back_local, back_send, back_recv, sum_send, sum_recv = refs
+    me, row = lax.axis_index("ctx"), lax.axis_index("seq")
+    head = total.shape[2]
+    mesh_id = pl.DeviceIdType.MESH
+
+    barrier = pltpu.get_barrier_semaphore()
+    for d in range(1, n):
+        pl.semaphore_signal(barrier, 1, device_id=(row, lax.rem(me + d, n)), device_id_type=mesh_id)
+    for d in range(1, seqs):
+        pl.semaphore_signal(barrier, 1, device_id=(lax.rem(row + d, seqs), me), device_id_type=mesh_id)
+
+    def columns(device, h):
+        return pl.ds(pl.multiple_of((device * own + h) * head, head), head)
+
+    def own_in(h, i):
+        return pltpu.make_async_copy(
+            args[i].at[:, columns(me, h)], recv.at[h, me, :, pl.ds(i * head, head)], local_sem.at[h, i]
+        )
+
+    def far_in(h, d, i):
+        to = lax.rem(me + d, n)
+        return pltpu.make_async_remote_copy(
+            src_ref=args[i].at[:, columns(to, h)],
+            dst_ref=recv.at[h, me, :, pl.ds(i * head, head)],
+            send_sem=out_send.at[h, d, i],
+            recv_sem=out_recv.at[h, d, i],
+            device_id=(row, to),
+            device_id_type=mesh_id,
+        )
+
+    def far_ids(d):
+        to = lax.rem(me + d, n)
+        return pltpu.make_async_remote_copy(
+            src_ref=ids.at[to],
+            dst_ref=recv_ids.at[me],
+            send_sem=ids_send.at[d],
+            recv_sem=ids_recv.at[d],
+            device_id=(row, to),
+            device_id_type=mesh_id,
+        )
+
+    def own_back(h, i):
+        return pltpu.make_async_copy(
+            ready.at[h, me, :, pl.ds(i * head, head)], grads[i].at[:, columns(me, h)], back_local.at[h, i]
+        )
+
+    def far_back(h, d, i):
+        to = lax.rem(me + d, n)
+        return pltpu.make_async_remote_copy(
+            src_ref=ready.at[h, to, :, pl.ds(i * head, head)],
+            dst_ref=grads[i].at[:, columns(me, h)],
+            send_sem=back_send.at[h, d, i],
+            recv_sem=back_recv.at[h, d, i],
+            device_id=(row, to),
+            device_id_type=mesh_id,
+        )
+
+    def far_sum(h, d):
+        return pltpu.make_async_remote_copy(
+            src_ref=all_sums.at[h, row],
+            dst_ref=all_sums.at[h, row],
+            send_sem=sum_send.at[h, d],
+            recv_sem=sum_recv.at[h, d],
+            device_id=(lax.rem(row + d, seqs), me),
+            device_id_type=mesh_id,
+        )
+
+    def over(low, high, act):
+        def step(d, carry):
+            act(d)
+            return carry
+
+        lax.fori_loop(low, high, step, 0)
+
+    def each(act, count):
+        for i in range(count):
+            act(i)
+
+    own_ids = pltpu.make_async_copy(ids.at[me], recv_ids.at[me], ids_local)
+    own_ids.start()
+    for h in range(own):
+        each(lambda i: own_in(h, i).start(), 4)
+    pl.semaphore_wait(barrier, n + seqs - 2)
+    over(1, n, lambda d: far_ids(d).start())
+    for h in range(own):
+        over(1, n, lambda d: each(lambda i: far_in(h, d, i).start(), 4))
     fill_tables(upper, causal)
-    sums[...] = jnp.zeros_like(sums)
-
-    def into(b, carry):
-        sums[...] += expand_block(x[b], ids[b], b, upper, slots, bias, slot_col.at[b])
-        return carry
-
-    lax.fori_loop(0, n, into, 0)
-    attend(slots, bias, causal, 4)
-
-    def back(b, carry):
-        def write(first, rows):
-            out[b, pl.ds(first, rows.shape[0]), :] = rows
-
-        collect_block(b, slots, slot_col.at[b], write)
-        return carry
-
-    lax.fori_loop(0, n, back, 0)
-
-
-def head_grads(x, ids, clusters):
-    n, tok, width = x.shape
-    head = width // 4
-    count = n * (2 * tok // clusters)
-    vmem = pl.BlockSpec(memory_space=pltpu.VMEM)
-    return pl.pallas_call(
-        head_kernel,
-        out_shape=(
-            jax.ShapeDtypeStruct((n, tok, 3 * head), jnp.bfloat16),
-            jax.ShapeDtypeStruct((clusters, head), jnp.float32),
-        ),
-        in_specs=[vmem, vmem],
-        out_specs=(vmem, vmem),
-        scratch_shapes=[
-            pltpu.VMEM((clusters, count, width), jnp.bfloat16),
-            pltpu.VMEM((clusters, count, 128), jnp.float32),
-            pltpu.VMEM((n, tok, 128), jnp.int32),
-            pltpu.VMEM((tok, tok), jnp.bfloat16),
-            pltpu.VMEM((count, count), jnp.float32),
-        ],
-        compiler_params=pltpu.CompilerParams(vmem_limit_bytes=60 * 1024 * 1024),
-        cost_estimate=pl.CostEstimate(flops=30_000_000_000, bytes_accessed=8 << 20, transcendentals=0),
-    )(x, ids)
+    own_ids.wait()
+
+    for h in range(own):
+
+        def expand(b):
+            sums[...] += expand_block(recv[h, b], recv_ids[b, h], b, upper, slots, bias, slot_col.at[b])
+
+        def arrive(d):
+            if h == 0:
+                far_ids(d).wait_recv()
+            each(lambda i: far_in(h, d, i).wait_recv(), 4)
+            expand(lax.rem(me - d + n, n))
+
+        def collect(b):
+            def write(first, rows):
+                ready[h, b, pl.ds(first, rows.shape[0]), :] = rows
+
+            collect_block(b, slots, slot_col.at[b], write)
+
+        def leave(d):
+            collect(lax.rem(me + d, n))
+            each(lambda i: far_back(h, d - 1, i).start(), 3)
+
+        sums[...] = jnp.zeros_like(sums)
+        each(lambda i: own_in(h, i).wait(), 4)
+        expand(me)
+        over(1, n, arrive)
+        all_sums[h, row] = sums[...].astype(jnp.bfloat16)
+        attend(slots, bias, causal, 4)
+        over(1, seqs, lambda d: far_sum(h, d).start())
+        collect(lax.rem(me + 1, n))
+        over(2, n, leave)
+        collect(me)
+        each(lambda i: far_back(h, n - 1, i).start(), 3)
+        each(lambda i: own_back(h, i).start(), 3)
+
+    for h in range(own):
+        over(1, seqs, lambda d: far_sum(h, d).wait())
+        whole = all_sums[h, 0].astype(jnp.float32)
+        for s in range(1, seqs):
+            whole = whole + all_sums[h, s].astype(jnp.float32)
+        total[h] = whole
+    over(1, n, lambda d: far_ids(d).wait_send())
+    for h in range(own):
+        over(1, n, lambda d: each(lambda i: far_in(h, d, i).wait_send(), 4))
+        each(lambda i: own_back(h, i).wait(), 3)
+        over(1, n, lambda d: each(lambda i: far_back(h, d, i).wait(), 3))
 
 
 def shards(queries, keys, values, out_grad, cluster_ids, centroids):
@@ -153,27 +246,45 @@
     n = lax.axis_size("ctx")
     seqs = lax.axis_size("seq")
     own = heads // n
-    a2a = functools.partial(lax.all_to_all, axis_name="ctx", split_axis=0, concat_axis=0, tiled=True)
-    ids = a2a(cluster_ids.reshape(n, own, tok)).reshape(n, own, 1, tok)
-    split = [a[0].reshape(tok, n, own, head) for a in (queries, keys, values, out_grad)]
-    arrived = [
-        a2a(jnp.transpose(jnp.concatenate([a[:, :, h] for a in split], axis=-1), (1, 0, 2)))
-        for h in range(own)
-    ]
-    done = [head_grads(arrived[h], ids[:, h], clusters) for h in range(own)]
-    back = jnp.stack([a2a(d[0]) for d in done], axis=1)
-    sums = jnp.stack([d[1] for d in done]).astype(jnp.bfloat16)
-    total = sums.astype(jnp.float32)
-    for d in range(1, seqs):
-        moved = lax.ppermute(sums, "seq", [(i, (i + d) % seqs) for i in range(seqs)])
-        total = total + moved.astype(jnp.float32)
+    count = n * (2 * tok // clusters)
+    dma = pltpu.SemaphoreType.DMA
+    anywhere = pl.BlockSpec(memory_space=pl.ANY)
+    *grads, total = pl.pallas_call(
+        functools.partial(spread_kernel, n, seqs, own),
+        out_shape=[jax.ShapeDtypeStruct((tok, heads * head), jnp.bfloat16)] * 3
+        + [jax.ShapeDtypeStruct((own, clusters, head), jnp.float32)],
+        in_specs=[anywhere] * 5,
+        out_specs=[anywhere] * 3 + [pl.BlockSpec(memory_space=pltpu.VMEM)],
+        scratch_shapes=[
+            pltpu.VMEM((own, n, tok, 4 * head), jnp.bfloat16),
+            pltpu.VMEM((n, own, 1, tok), jnp.int32),
+            pltpu.VMEM((own, n, tok, 3 * head), jnp.bfloat16),
+            pltpu.VMEM((own, seqs, clusters, head), jnp.bfloat16),
+            pltpu.VMEM((clusters, head), jnp.float32),
+            pltpu.VMEM((clusters, count, 4 * head), jnp.bfloat16),
+            pltpu.VMEM((clusters, count, 128), jnp.float32),
+            pltpu.VMEM((n, tok, 128), jnp.int32),
+            pltpu.VMEM((tok, tok), jnp.bfloat16),
+            pltpu.VMEM((count, count), jnp.float32),
+            dma((own, 4)),
+            dma,
+            dma((own, n, 4)),
+            dma((own, n, 4)),
+            dma((n,)),
+            dma((n,)),
+            dma((own, 3)),
+            dma((own, n, 3)),
+            dma((own, n, 3)),
+            dma((own, seqs)),
+            dma((own, seqs)),
+        ],
+        compiler_params=pltpu.CompilerParams(
+            collective_id=0, has_side_effects=True, vmem_limit_bytes=60 * 1024 * 1024
+        ),
+    )(queries[0], keys[0], values[0], out_grad[0], cluster_ids.reshape(n, own, 1, tok))
     centroid_own = lax.dynamic_slice_in_dim(centroids, lax.axis_index("ctx") * own, own, 0)
     updated = decay_rate * centroid_own + (1.0 - decay_rate) / 2.0 * total
-    per_token = jnp.transpose(back, (2, 0, 1, 3))
-    grads = [
-        per_token[..., i * head : (i + 1) * head].reshape(1, tok, heads * head) for i in range(3)
-    ]
-    return (*grads, updated)
+    return (*[a[None] for a in grads], updated)
 
 
 def solution(mesh):

time: 251 us -> 177 us (0.71)
  Pallas kernels: 54.1 us -> 166 us
  waiting for transfers between devices: 103 us -> 0 us
  local copies, waits for them, and re-layouts: 50.9 us -> 6.98 us
  starting transfers between devices: 29 us -> 0 us
  other arithmetic: 11.9 us -> 1.52 us
    pallas_call x2 -> x1, Pallas kernels: 54.1 us -> 166 us  [shards(): pl.pallas_call(functools.partial(spread_kernel, n, seqs, own), out_shape=...]
    all_to_all x5 -> x0, waiting for transfers between devices: 101 us -> none  [the longest x2 62.5 us: shards(): a2a(jnp.transpose(jnp.concatenate([a[:, :, h] for a in split], axis=-1),...]
    unnamed x27 -> x7, local copies, waits for them, and re-layouts: 31.6 us -> 6.98 us
    all_to_all x5 -> x0, starting transfers between devices: 22.6 us -> none  [the longest x2 9.26 us: shards(): a2a(jnp.transpose(jnp.concatenate([a[:, :, h] for a in split], axis=-1),...]
    slice x8 -> x0, local copies, waits for them, and re-layouts: 17.9 us -> none  [the longest x4 12.1 us: shards(): per_token[..., i * head:(i + 1) * head].reshape(1, tok, heads * head)]
    transpose x3 -> x0, other arithmetic: 9.57 us -> none  [the longest x2 6.98 us: shards(): jnp.transpose(jnp.concatenate([a[:, :, h] for a in split], axis=-1), (1,...]
    ppermute x3 -> x0, starting transfers between devices: 6.48 us -> none  [shards(): lax.ppermute(sums, 'seq', [(i, (i + d) % seqs) for i in range(seqs)])]
  transfers between devices with their start and end apart: 8 -> 0, of which waited for: 5 -> 0; matrix products, arithmetic and copies ran while one was open for 16% -> 0% of each run, Pallas kernels for 22% -> 0%
where the time goes in v2:
time: 177 us; the launch traced here: 175 us
  Pallas kernels  166 us (94%)
  local copies, waits for them, and re-layouts  6.98 us (4%)
    pallas_call x1, Pallas kernels, shards(): pl.pallas_call(functools.partial(spread_kernel, n, seqs, own), out_shape=...  166 us
    unnamed x7, local copies, waits for them, and re-layouts  6.98 us

profile of v2, /device:TPU:0, one launch (start us, length us, event | category | flops | bytes accessed | tf_op | source)
XLA Modules:
  0.0 175.3 jit_solution(16244715888639632181)
XLA Ops:
  0.6 166.1 %shard_map.93 = (bf16[512,2048]{1,0:T(8,128)(2,1)}, bf16[512,2048]{1,0:T(8,128)(2,1)}, bf16[512,2048]{1,0:T(8,128)(2,1)}, f32[2,64,128]{2,1,0:T(8,128)}) custom-call(bf16[512,2048]{1,0:T(8,128)(2,1)} %bitcast.11, bf16[512,2048]{1,0:T(8,128)(2,1)} %bitcast.12, bf16[512,2048]{1,0:T(8,128)(2,1)} %bitcast.13, bf16[512,2048]{1,0:T(8,128)(2,1)} %bitcast.14, ...), custom_call_target="tpu_custom_call" | custom-call | tf_op jit(solution)/shard_map/pallas_call | solution.py:252
  166.8 1.5 multiply_add_fusion
  168.3 0.0 copy-start.1
  168.3 3.3 %copy.13 = bf16[1,512,2048]{2,1,0:T(8,128)(2,1)} copy(bf16[1,512,2048]{2,1,0:T(8,128)(2,1)} %bitcast.10) | data formatting | bytes 4194304
  171.6 0.0 copy-done.1
  171.6 0.0 copy-start
  171.6 1.3 copy.14
  172.9 1.0 copy-done
  174.0 1.3 copy.15
Async XLA Ops:
  168.3 3.3 %copy-start.1 = (bf16[512,2048]{1,0:T(8,128)(2,1)S(1)}, bf16[512,2048]{1,0:T(8,128)(2,1)}, u32[]{:S(2)}) copy-start(bf16[512,2048]{1,0:T(8,128)(2,1)} %get-tuple-element.9) | copy-start | bytes 6291460
  171.6 2.3 %copy-start = (bf16[512,2048]{1,0:T(8,128)(2,1)S(1)}, bf16[512,2048]{1,0:T(8,128)(2,1)}, u32[]{:S(2)}) copy-start(bf16[512,2048]{1,0:T(8,128)(2,1)} %get-tuple-element.10) | copy-start | bytes 6291460

commit v3 on v2

--- a/solution.py
+++ b/solution.py
@@ -118,14 +118,14 @@
 
     def own_in(h, i):
         return pltpu.make_async_copy(
-            args[i].at[:, columns(me, h)], recv.at[h, me, :, pl.ds(i * head, head)], local_sem.at[h, i]
+            args[i].at[:, columns(me, h)], recv.at[h, me, i], local_sem.at[h, i]
         )
 
     def far_in(h, d, i):
         to = lax.rem(me + d, n)
         return pltpu.make_async_remote_copy(
             src_ref=args[i].at[:, columns(to, h)],
-            dst_ref=recv.at[h, me, :, pl.ds(i * head, head)],
+            dst_ref=recv.at[h, me, i],
             send_sem=out_send.at[h, d, i],
             recv_sem=out_recv.at[h, d, i],
             device_id=(row, to),
@@ -145,13 +145,13 @@
 
     def own_back(h, i):
         return pltpu.make_async_copy(
-            ready.at[h, me, :, pl.ds(i * head, head)], grads[i].at[:, columns(me, h)], back_local.at[h, i]
+            ready.at[h, me, i], grads[i].at[:, columns(me, h)], back_local.at[h, i]
         )
 
     def far_back(h, d, i):
         to = lax.rem(me + d, n)
         return pltpu.make_async_remote_copy(
-            src_ref=ready.at[h, to, :, pl.ds(i * head, head)],
+            src_ref=ready.at[h, to, i],
             dst_ref=grads[i].at[:, columns(me, h)],
             send_sem=back_send.at[h, d, i],
             recv_sem=back_recv.at[h, d, i],
@@ -194,7 +194,7 @@
     for h in range(own):
 
         def expand(b):
-            sums[...] += expand_block(recv[h, b], recv_ids[b, h], b, upper, slots, bias, slot_col.at[b])
+            sums[...] += expand_block(jnp.concatenate([recv[h, b, i] for i in range(4)], axis=1), recv_ids[b, h], b, upper, slots, bias, slot_col.at[b])
 
         def arrive(d):
             if h == 0:
@@ -204,7 +204,8 @@
 
         def collect(b):
             def write(first, rows):
-                ready[h, b, pl.ds(first, rows.shape[0]), :] = rows
+                for i in range(3):
+                    ready[h, b, i, pl.ds(first, rows.shape[0]), :] = rows[:, i * head : (i + 1) * head]
 
             collect_block(b, slots, slot_col.at[b], write)
 
@@ -256,9 +257,9 @@
         in_specs=[anywhere] * 5,
         out_specs=[anywhere] * 3 + [pl.BlockSpec(memory_space=pltpu.VMEM)],
         scratch_shapes=[
-            pltpu.VMEM((own, n, tok, 4 * head), jnp.bfloat16),
+            pltpu.VMEM((own, n, 4, tok, head), jnp.bfloat16),
             pltpu.VMEM((n, own, 1, tok), jnp.int32),
-            pltpu.VMEM((own, n, tok, 3 * head), jnp.bfloat16),
+            pltpu.VMEM((own, n, 3, tok, head), jnp.bfloat16),
             pltpu.VMEM((own, seqs, clusters, head), jnp.bfloat16),
             pltpu.VMEM((clusters, head), jnp.float32),
             pltpu.VMEM((clusters, count, 4 * head), jnp.bfloat16),

time: 177 us -> 177 us (level)
  no operation moved by 1% of the time
where the time goes in v3:
time: 177 us; the launch traced here: 175 us
  Pallas kernels  166 us (94%)
  local copies, waits for them, and re-layouts  6.98 us (4%)
    pallas_call x1, Pallas kernels, shards(): pl.pallas_call(functools.partial(spread_kernel, n, seqs, own), out_shape=...  166 us
    unnamed x7, local copies, waits for them, and re-layouts  6.98 us

profile of v3, /device:TPU:0, one launch (start us, length us, event | category | flops | bytes accessed | tf_op | source)
XLA Modules:
  0.0 175.3 jit_solution(16952089730546864353)
XLA Ops:
  0.6 166.1 %shard_map.93 = (bf16[512,2048]{1,0:T(8,128)(2,1)}, bf16[512,2048]{1,0:T(8,128)(2,1)}, bf16[512,2048]{1,0:T(8,128)(2,1)}, f32[2,64,128]{2,1,0:T(8,128)}) custom-call(bf16[512,2048]{1,0:T(8,128)(2,1)} %bitcast.11, bf16[512,2048]{1,0:T(8,128)(2,1)} %bitcast.12, bf16[512,2048]{1,0:T(8,128)(2,1)} %bitcast.13, bf16[512,2048]{1,0:T(8,128)(2,1)} %bitcast.14, ...), custom_call_target="tpu_custom_call" | custom-call | tf_op jit(solution)/shard_map/pallas_call | solution.py:253
  166.8 1.5 multiply_add_fusion
  168.3 0.0 copy-start.1
  168.3 3.3 %copy.13 = bf16[1,512,2048]{2,1,0:T(8,128)(2,1)} copy(bf16[1,512,2048]{2,1,0:T(8,128)(2,1)} %bitcast.10) | data formatting | bytes 4194304
  171.6 0.0 copy-done.1
  171.6 0.0 copy-start
  171.6 1.3 copy.14
  172.9 1.0 copy-done
  174.0 1.3 copy.15
Async XLA Ops:
  168.3 3.3 %copy-start.1 = (bf16[512,2048]{1,0:T(8,128)(2,1)S(1)}, bf16[512,2048]{1,0:T(8,128)(2,1)}, u32[]{:S(2)}) copy-start(bf16[512,2048]{1,0:T(8,128)(2,1)} %get-tuple-element.9) | copy-start | bytes 6291460
  171.6 2.3 %copy-start = (bf16[512,2048]{1,0:T(8,128)(2,1)S(1)}, bf16[512,2048]{1,0:T(8,128)(2,1)}, u32[]{:S(2)}) copy-start(bf16[512,2048]{1,0:T(8,128)(2,1)} %get-tuple-element.10) | copy-start | bytes 6291460
